TPU v7x, 32 devices: a whole 2x2x4 slice. The times are simulated.
32 devices in a mesh: groups: 2 (over x), replica: 2 (over core), tensor: 8 (over z, y).
Axes of the slice: x: 2, y: 2, z: 4, core: 2. Of those that a mesh axis runs over, the one named last changes fastest.
Arguments:
- hidden: bfloat16 [128, 8192], P(('groups', 'replica'), 'tensor'), parts along dimension 0, may hold values from -6 to 6
- w_query: bfloat16 [8192, 8192], P(None, 'tensor'), may hold values from -0.0625 to 0.0625
- output_weight: bfloat16 [8192, 8192], P('tensor'), may hold values from -0.09375 to 0.09375
- keys: bfloat16 [128, 8, 32, 128], P(('groups', 'replica')), parts along dimension 0
- values: bfloat16 [128, 8, 32, 128], P(('groups', 'replica')), parts along dimension 0, may hold values from -6 to 6
- query_down_maps: bfloat16 [16, 64, 8192], P(('groups', 'replica'), None, 'tensor'), parts along dimension 0, may hold values from -0.0625 to 0.0625
- query_up_maps: bfloat16 [16, 64, 8192], P(('groups', 'replica'), None, 'tensor'), parts along dimension 0, may hold values from -0.75 to 0.75
- output_down_maps: bfloat16 [16, 64, 8192], P(('groups', 'replica'), None, 'tensor'), parts along dimension 0, may hold values from -0.0625 to 0.0625
- output_up_maps: bfloat16 [16, 64, 8192], P(('groups', 'replica'), None, 'tensor'), parts along dimension 0, may hold values from -0.75 to 0.75
- adapter_ids: int32 [128], P('groups'), parts along dimension 0, may hold values from 0 to 7
- owner_map: int32 [16], P('groups'), parts along dimension 0, may hold values from 0 to 7, each once
- kv_lengths: int32 [128], P(('groups', 'replica')), parts along dimension 0, may hold values from 1 to 32, as said below
Outputs:
- attn_out: bfloat16 [128, 8192], P(('groups', 'replica'), 'tensor'), parts along dimension 0
There are 2 independent parts, one for each index of `groups`. A program takes and returns all parts, laid end to end along the dimension named above; an argument that names none is the same for every part. Nothing has to cross between parts.
Inputs may be any that keep to these rules, and one draw needn't show every extreme that they name: `owner_map`: every request's adapter has a slot; slot s is stored at replica index s // 4. Request r attends to its first kv_lengths[r] cached positions; some request holds all 32.
All inputs are finite; a program needn't handle non-finite values.
Results may differ from a plain program's by a relative error of at most 0.0092.
Values may be sent and summed in bfloat16 or wider, within the bound.
No kernel may reach another device: no remote copies, remote signals or barrier semaphores. Data moves between devices by JAX's collectives and lax.ppermute only.
A program may use at most 128 MiB of HBM per device.

v0:
```python
import math
import jax
import jax.numpy as jnp
from jax import lax
from jax.sharding import PartitionSpec as P

HEADS = 64
KVS = 8


def adapt(input_rows, slots, down_product, up_product):
    stored = down_product.shape[0]
    table = lax.broadcasted_iota(jnp.int32, (1, stored), 1)
    pick = (slots[:, None] == table).astype(jnp.bfloat16)
    part = jnp.einsum("ah,fth->aft", input_rows, down_product, preferred_element_type=jnp.float32)
    partial_value = jnp.sum(pick.astype(jnp.float32)[:, :, None] * part, axis=1)
    total = lax.psum(partial_value, "tensor")
    low = total.astype(jnp.bfloat16)
    spread_rows = pick[:, :, None] * low[:, None, :]
    return jnp.einsum("xpl,ply->xy", spread_rows, up_product, preferred_element_type=jnp.float32)


def per_device(
    hidden,
    w_query,
    output_weight,
    keys,
    values,
    query_down_maps,
    query_up_maps,
    output_down_maps,
    output_up_maps,
    adapter_ids,
    owner_map,
    kv_lengths,
):
    rows = hidden.shape[0]
    head_size = keys.shape[3]
    replica_at = lax.axis_index("replica")
    tensor_at = lax.axis_index("tensor")
    id_table = lax.broadcasted_iota(jnp.int32, (1, owner_map.shape[0]), 1)
    slots_all = jnp.sum(jnp.where(adapter_ids[:, None] == id_table, owner_map[None, :], 0), axis=1)
    own_slots = lax.dynamic_slice_in_dim(slots_all, replica_at * rows, rows)
    query_down_maps, query_up_maps, output_down_maps, output_up_maps = (
        lax.all_gather(query_down_maps, "replica", axis=0, tiled=True),
        lax.all_gather(query_up_maps, "replica", axis=0, tiled=True),
        lax.all_gather(output_down_maps, "replica", axis=0, tiled=True),
        lax.all_gather(output_up_maps, "replica", axis=0, tiled=True),
    )

    def apply_adapter(input_rows, down_product, up_product):
        return adapt(input_rows, own_slots, down_product, up_product)

    plain_projection = jnp.dot(
        lax.all_gather(hidden, "tensor", axis=1, tiled=True),
        w_query,
        preferred_element_type=jnp.float32,
    )
    query_rows = (
        plain_projection + 0.5 * apply_adapter(hidden, query_down_maps, query_up_maps)
    ).astype(jnp.bfloat16)
    local_heads = query_rows.shape[1] // head_size
    group = HEADS // KVS
    kv_count = max(1, local_heads // group)
    first_kv = tensor_at * local_heads // group
    key_block = lax.dynamic_slice_in_dim(keys, first_kv, kv_count, 1)
    value_block = lax.dynamic_slice_in_dim(values, first_kv, kv_count, 1)
    heads_q = query_rows.reshape(rows, kv_count, local_heads // kv_count, head_size)
    scores = jnp.einsum(
        "rkhd,rkld->rkhl", heads_q, key_block, preferred_element_type=jnp.float32
    ) / math.sqrt(head_size)
    live = (
        lax.broadcasted_iota(jnp.int32, (rows, 1, 1, keys.shape[2]), 3)
        < kv_lengths[:, None, None, None]
    )
    scores = jnp.where(live, scores, -1e30)
    top = jnp.max(scores, axis=-1, keepdims=True)
    weights = jnp.exp(scores - top)
    probs = (weights / jnp.sum(weights, axis=-1, keepdims=True)).astype(jnp.bfloat16)
    combined_output = jnp.einsum(
        "rkhl,rkld->rkhd", probs, value_block, preferred_element_type=jnp.float32
    )
    combined_output = combined_output.astype(jnp.bfloat16).reshape(rows, -1)
    partial_value = jnp.dot(combined_output, output_weight, preferred_element_type=jnp.float32)
    out_base = lax.psum_scatter(partial_value, "tensor", scatter_dimension=1, tiled=True)
    final_output = out_base + 0.5 * apply_adapter(combined_output, output_down_maps, output_up_maps)
    return final_output.astype(jnp.bfloat16)


def solution(mesh):
    return jax.shard_map(
        per_device,
        mesh=mesh,
        in_specs=(
            P(("groups", "replica"), "tensor"),
            P(None, "tensor"),
            P("tensor", None),
            P(("groups", "replica"), None, None, None),
            P(("groups", "replica"), None, None, None),
            P(("groups", "replica"), None, "tensor"),
            P(("groups", "replica"), None, "tensor"),
            P(("groups", "replica"), None, "tensor"),
            P(("groups", "replica"), None, "tensor"),
            P("groups"),
            P("groups"),
            P(("groups", "replica")),
        ),
        out_specs=P(("groups", "replica"), "tensor"),
        check_vma=False,
    )
```

profile of v0, /device:TPU:0, one launch (start us, length us, event | category | flops | bytes accessed | tf_op | source)
XLA Modules:
  0.0 174.8 jit_solution(11398326931381532155)
XLA Ops:
  6.5 0.0 all-gather.5.cloned.1.call-start
  6.6 0.7 all-gather.5.cloned.1.call-update
  7.3 0.0 all-gather.7.cloned.1.call-start
  7.3 0.7 all-gather.7.cloned.1.call-update
  8.0 0.0 all-gather.9.cloned.1.call-start
  8.1 0.7 all-gather.9.cloned.1.call-update
  8.8 0.0 all-gather.11.cloned.1.call-start
  8.8 0.5 all-gather.11.cloned.1.call-update
  9.3 0.0 reduce-scatter.2.cloned.1.call-start
  9.4 0.1 select_reduce_fusion
  9.5 0.1 dynamic_slice.9
  9.6 33.0 %all_gather.15 = bf16[32,8192]{1,0:T(8,128)(2,1)S(1)} all-gather(bf16[32,1024]{1,0:T(8,128)(2,1)S(1)} %copy-done.1), channel_id=1, replica_groups=mesh['groups'=2,'replica'=2,'tensor'=8] {'tensor'}, dimensions={1}, use_global_device_ids=true | all-gather | bytes 589824 | tf_op jit(solution)/shard_map/all_gather | solution.py:55
  42.6 0.1 iota_compare_fusion
  42.7 8.7 %fusion.55 = f32[32,1024]{1,0:T(8,128)S(1)} fusion(bf16[32,8192]{1,0:T(8,128)(2,1)S(1)} %all_gather.15, bf16[8192,1024]{1,0:T(8,128)(2,1)} %param.13), kind=kOutput, calls=%fused_computation.51 | convolution fusion | flops 536870912 | bytes 17432576 | tf_op jit(solution)/shard_map/dot_general | solution.py:54
  51.5 1.8 %fusion.10 = f32[32,64]{1,0:T(8,128)S(1)} fusion(bf16[8,64,1024]{2,1,0:T(8,128)(2,1)} %all-gather.5.cloned.1.call-done, bf16[32,1024]{1,0:T(8,128)(2,1)S(1)} %copy-done.1, f32[32,8]{0,1:T(8,128)S(1)} %get-tuple-element.6), kind=kOutput, calls=%fused_computation.16 | convolution fusion | flops 33585152 | bytes 1123328 | tf_op jit(solution)/shard_map/ah,fth->aft/dot_general | solution.py:15
  53.3 37.4 %psum.14 = bf16[32,64]{1,0:T(8,128)(2,1)S(1)} all-reduce(f32[32,64]{1,0:T(8,128)S(1)} %fusion.10), channel_id=1, replica_groups=mesh['groups'=2,'replica'=2,'tensor'=8] {'tensor'}, use_global_device_ids=true, to_apply=%region_2.3 | all-reduce | flops 2048 | bytes 12288 | tf_op jit(solution)/shard_map/psum | solution.py:17
  90.7 1.6 fusion.12
  92.3 0.4 fusion.52
  92.8 1.5 convolution_convert_fusion
  94.3 9.8 %fusion.17 = f32[32,8192]{1,0:T(8,128)} fusion(bf16[1024,8192]{1,0:T(8,128)(2,1)} %param.14, bf16[4,8,8,128]{3,2,1,0:T(8,128)(2,1)S(1)} %bitcast.54), kind=kOutput, calls=%fused_computation.24 | convolution fusion | flops 536870912 | bytes 17891328 | tf_op jit(solution)/shard_map/dot_general | solution.py:84
  104.1 1.8 %fusion.11 = f32[32,64]{1,0:T(8,128)S(1)} fusion(bf16[32,1024,1]{1,0,2:T(8,128)(2,1)S(1)} %reshape.106, bf16[8,64,1024]{2,1,0:T(8,128)(2,1)} %all-gather.9.cloned.1.call-done, f32[32,8]{0,1:T(8,128)S(1)} %get-tuple-element.6), kind=kOutput, calls=%fused_computation.17 | convolution fusion | flops 33585152 | bytes 1123328 | tf_op jit(solution)/shard_map/ah,fth->aft/dot_general | solution.py:15
  106.0 33.3 %psum.15 = bf16[32,64]{1,0:T(8,128)(2,1)S(1)} all-reduce(f32[32,64]{1,0:T(8,128)S(1)} %fusion.11), channel_id=1, replica_groups=mesh['groups'=2,'replica'=2,'tensor'=8] {'tensor'}, use_global_device_ids=true, to_apply=%region_7.8 | all-reduce | flops 2048 | bytes 12288 | tf_op jit(solution)/shard_map/psum | solution.py:17
  139.2 26.8 %reduce-scatter.2.cloned.1.call-done = f32[32,1024]{1,0:T(8,128)} async-done(((f32[32,8192]{1,0:T(8,128)}), f32[32,1024]{1,0:T(8,128)}) %reduce-scatter.2.cloned.1.call-update) | async-done | bytes 131088 | tf_op jit(solution)/shard_map/reduce_scatter | solution.py:85
  166.1 2.2 %fusion.8 = bf16[32,1024]{1,0:T(8,128)(2,1)} fusion(f32[32,1024]{1,0:T(8,128)} %reduce-scatter.2.cloned.1.call-done, bf16[8,64,1024]{2,1,0:T(8,128)(2,1)} %all-gather.11.cloned.1.call-done, bf16[32,64]{1,0:T(8,128)(2,1)S(1)} %psum.15, bf16[32,8]{0,1:T(8,128)(2,1)S(1)} %get-tuple-element.5), kind=kOutput, calls=%fused_computation.13 | convolution fusion | flops 33669120 | bytes 1249792 | tf_op jit(solution)/shard_map/xpl,ply->xy/dot_general | solution.py:20
  (18 shorter events, 0.1 us)
Async XLA Ops:
  6.5 85.8 %copy-start = (bf16[32,8,32,128]{3,2,1,0:T(8,128)(2,1)S(1)}, bf16[32,8,32,128]{3,2,1,0:T(8,128)(2,1)}, u32[]{:S(2)}) copy-start(bf16[32,8,32,128]{3,2,1,0:T(8,128)(2,1)} %param.15) | copy-start | bytes 6291460
  6.5 2.9 %copy-start.4 = (s32[64]{0:T(128)S(1)}, s32[64]{0:T(128)}, u32[]{:S(2)}) copy-start(s32[64]{0:T(128)} %param.21) | copy-start | bytes 772
  6.5 2.9 %copy-start.3 = (s32[8]{0:T(128)S(1)}, s32[8]{0:T(128)}, u32[]{:S(2)}) copy-start(s32[8]{0:T(128)} %param.22) | copy-start | bytes 100
  6.5 3.1 %copy-start.1 = (bf16[32,1024]{1,0:T(8,128)(2,1)S(1)}, bf16[32,1024]{1,0:T(8,128)(2,1)}, u32[]{:S(2)}) copy-start(bf16[32,1024]{1,0:T(8,128)(2,1)} %param.12) | copy-start | bytes 196612
  6.5 36.1 %copy-start.2 = (s32[32]{0:T(128)S(1)}, s32[32]{0:T(128)}, u32[]{:S(2)}) copy-start(s32[32]{0:T(128)} %param.23) | copy-start | bytes 388
  6.5 44.9 %all-gather.5.cloned.1.call-start = ((), (), s32[]{:S(2)}) async-start(), calls=%async_computation.1 | async-start | bytes 1572864 | tf_op jit(solution)/shard_map/all_gather | solution.py:45
  7.3 83.4 %all-gather.7.cloned.1.call-start = ((), (), s32[]{:S(2)}) async-start(), calls=%async_computation.2 | async-start | bytes 1572864 | tf_op jit(solution)/shard_map/all_gather | solution.py:46
  8.0 96.1 %all-gather.9.cloned.1.call-start = ((), (), s32[]{:S(2)}) async-start(), calls=%async_computation.4 | async-start | bytes 1572864 | tf_op jit(solution)/shard_map/all_gather | solution.py:47
  8.8 130.4 %all-gather.11.cloned.1.call-start = ((), (), s32[]{:S(2)}) async-start(), calls=%async_computation.5 | async-start | bytes 1572864 | tf_op jit(solution)/shard_map/all_gather | solution.py:48
  9.3 156.7 %reduce-scatter.2.cloned.1.call-start = ((), (), s32[]{:S(2)}) async-start(), calls=%async_computation.3 | async-start | bytes 1179648 | tf_op jit(solution)/shard_map/reduce_scatter | solution.py:85
Sparse Core Ops, SparseCore 0:
  8.9 11.7 all-gather.4
  22.2 10.1 all-gather.6
  34.0 10.1 all-gather.8
  45.6 10.2 all-gather.10
  104.2 61.8 reduce-scatter.1
where the time goes:
time: 175 us
  blocking collectives  104 us (59%)
  waiting for transfers between devices  29.5 us (17%)
  matrix products  28 us (16%)
  between operations  13.2 us (8%)
    psum x2, blocking collectives, adapt(): total = lax.psum(partial_value, 'tensor')  70.6 us
    all_gather x1, blocking collectives, per_device(): lax.all_gather(hidden, 'tensor', axis=1, tiled=True)  33 us
    reduce_scatter x1, waiting for transfers between devices, per_device(): lax.psum_scatter(partial_value, 'tensor', scatter_dimension=1, tiled=True)  26.8 us
    dot_general x1, matrix products, per_device(): jnp.dot(combined_output, output_weight, preferred_element_type=jnp.float32)  9.75 us
    dot_general x1, matrix products, per_device(): jnp.dot(lax.all_gather(hidden, 'tensor', axis=1, tiled=True), w_query, pr...  8.75 us
    dot_general x2, matrix products, adapt(): jnp.einsum('xpl,ply->xy', spread_rows, up_product, preferred_element_type...  3.86 us
    dot_general x2, matrix products, adapt(): jnp.einsum('ah,fth->aft', input_rows, down_product, preferred_element_typ...  3.67 us
  transfers between devices with their start and end apart: 5, of which 1 were waited for; matrix products, arithmetic and copies ran while one was open for 15% of the time, Pallas kernels for 0%

commit v1 on v0

--- a/solution.py
+++ b/solution.py
@@ -14,7 +14,9 @@
     pick = (slots[:, None] == table).astype(jnp.bfloat16)
     part = jnp.einsum("ah,fth->aft", input_rows, down_product, preferred_element_type=jnp.float32)
     partial_value = jnp.sum(pick.astype(jnp.float32)[:, :, None] * part, axis=1)
-    total = lax.psum(partial_value, "tensor")
+    total = partial_value
+    for hop in (1, 2, 4):
+        total = total + lax.ppermute(total, "tensor", [(dev, dev ^ hop) for dev in range(8)])
     low = total.astype(jnp.bfloat16)
     spread_rows = pick[:, :, None] * low[:, None, :]
     return jnp.einsum("xpl,ply->xy", spread_rows, up_product, preferred_element_type=jnp.float32)

time: 175 us -> 157 us (0.90)
  blocking collectives: 104 us -> 31.5 us
  waiting for transfers between devices: 29.5 us -> 74.8 us
  starting transfers between devices: 0.19 us -> 8.88 us
    psum x2 -> x0, blocking collectives: 70.6 us -> none  [adapt(): total = lax.psum(partial_value, 'tensor')]
    reduce_scatter x1, waiting for transfers between devices: 26.8 us -> 51 us  [per_device(): lax.psum_scatter(partial_value, 'tensor', scatter_dimension=1, tiled=True)]
    all_gather x1, waiting for transfers between devices: 0.01 us -> 11.1 us  [per_device(): lax.all_gather(query_down_maps, 'replica', axis=0, tiled=True)]
    ppermute x0 -> x6, waiting for transfers between devices: none -> 10 us  [adapt(): lax.ppermute(total, 'tensor', [(dev, dev ^ hop) for dev in range(8)])]
    ppermute x0 -> x6, starting transfers between devices: none -> 8.7 us  [adapt(): lax.ppermute(total, 'tensor', [(dev, dev ^ hop) for dev in range(8)])]
  transfers between devices with their start and end apart: 5 -> 11, of which waited for: 1 -> 6; matrix products, arithmetic and copies ran while one was open for 15% -> 17% of each run, Pallas kernels for 0% -> 0%
where the time goes in v1:
time: 157 us
  waiting for transfers between devices  74.8 us (48%)
  blocking collectives  31.5 us (20%)
  matrix products  28 us (18%)
  between operations  13.3 us (8%)
  starting transfers between devices  8.88 us (6%)
    reduce_scatter x1, waiting for transfers between devices, per_device(): lax.psum_scatter(partial_value, 'tensor', scatter_dimension=1, tiled=True)  51 us
    all_gather x1, blocking collectives, per_device(): lax.all_gather(hidden, 'tensor', axis=1, tiled=True)  31.5 us
    all_gather x1, waiting for transfers between devices, per_device(): lax.all_gather(query_down_maps, 'replica', axis=0, tiled=True)  11.1 us
    ppermute x6, waiting for transfers between devices, adapt(): lax.ppermute(total, 'tensor', [(dev, dev ^ hop) for dev in range(8)])  10 us
    dot_general x1, matrix products, per_device(): jnp.dot(combined_output, output_weight, preferred_element_type=jnp.float32)  9.77 us
    dot_general x1, matrix products, per_device(): jnp.dot(lax.all_gather(hidden, 'tensor', axis=1, tiled=True), w_query, pr...  8.75 us
    ppermute x6, starting transfers between devices, adapt(): lax.ppermute(total, 'tensor', [(dev, dev ^ hop) for dev in range(8)])  8.7 us
    dot_general x2, matrix products, adapt(): jnp.einsum('xpl,ply->xy', spread_rows, up_product, preferred_element_type...  3.87 us
  transfers between devices with their start and end apart: 11, of which 6 were waited for; matrix products, arithmetic and copies ran while one was open for 17% of the time, Pallas kernels for 0%

profile of v1, /device:TPU:0, one launch (start us, length us, event | category | flops | bytes accessed | tf_op | source)
XLA Modules:
  0.0 156.8 jit_solution(5544614882770334121)
XLA Ops:
  6.6 0.7 all-gather.5.cloned.1.call-update
  7.3 0.7 all-gather.7.cloned.1.call-update
  8.1 0.7 all-gather.9.cloned.1.call-update
  8.8 0.5 all-gather.11.cloned.1.call-update
  9.6 11.1 %all-gather.5.cloned.1.call-done = bf16[8,64,1024]{2,1,0:T(8,128)(2,1)} async-done(((bf16[4,64,1024]{2,1,0:T(8,128)(2,1)}), bf16[8,64,1024]{2,1,0:T(8,128)(2,1)}) %all-gather.5.cloned.1.call-update) | async-done | bytes 1048592 | tf_op jit(solution)/shard_map/all_gather | solution.py:47
  20.7 1.8 %fusion.10 = f32[32,64]{1,0:T(8,128)S(1)} fusion(bf16[8,64,1024]{2,1,0:T(8,128)(2,1)} %all-gather.5.cloned.1.call-done, bf16[32,1024]{1,0:T(8,128)(2,1)S(1)} %copy-done.1, f32[32,8]{0,1:T(8,128)S(1)} %get-tuple-element.6), kind=kOutput, calls=%fused_computation.16 | convolution fusion | flops 33585152 | bytes 1123328 | tf_op jit(solution)/shard_map/ah,fth->aft/dot_general | solution.py:15
  22.5 1.8 %collective-permute-start = (f32[32,64]{1,0:T(8,128)S(1)}, f32[32,64]{1,0:T(8,128)S(1)}, u32[]{:S(2)}, u32[]{:S(2)}) collective-permute-start(f32[32,64]{1,0:T(8,128)S(1)} %fusion.10), channel_id=1, source_target_pairs={{0,1},{1,0},{2,3},{3,2},{4,5},{5,4},{6,7},{7,6},{8,9},{9,8},{10,11... | collective-permute-start | bytes 24584 | tf_op jit(solution)/shard_map/ppermute | solution.py:19
  24.3 31.5 %all_gather.15 = bf16[32,8192]{1,0:T(8,128)(2,1)S(1)} all-gather(bf16[32,1024]{1,0:T(8,128)(2,1)S(1)} %copy-done.1), channel_id=1, replica_groups=mesh['groups'=2,'replica'=2,'tensor'=8] {'tensor'}, dimensions={1}, use_global_device_ids=true | all-gather | bytes 589824 | tf_op jit(solution)/shard_map/all_gather | solution.py:57
  55.9 8.7 %fusion.55 = f32[32,1024]{1,0:T(8,128)S(1)} fusion(bf16[32,8192]{1,0:T(8,128)(2,1)S(1)} %all_gather.15, bf16[8192,1024]{1,0:T(8,128)(2,1)} %param.13), kind=kOutput, calls=%fused_computation.53 | convolution fusion | flops 536870912 | bytes 17432576 | tf_op jit(solution)/shard_map/dot_general | solution.py:56
  64.7 1.2 collective-permute-start.2
  66.0 3.4 %collective-permute-done.2 = f32[32,64]{1,0:T(8,128)S(1)} collective-permute-done((f32[32,64]{1,0:T(8,128)S(1)}, f32[32,64]{1,0:T(8,128)S(1)}, u32[]{:S(2)}, u32[]{:S(2)}) %collective-permute-start.2) | collective-permute-done | bytes 8224 | tf_op jit(solution)/shard_map/ppermute | solution.py:19
  69.4 1.6 %fusion.12 = bf16[4,8,8,128]{3,1,2,0:T(8,128)(2,1)S(1)} fusion(f32[32,1024]{1,0:T(8,128)S(1)} %fusion.55, bf16[8,64,1024]{2,1,0:T(8,128)(2,1)} %all-gather.7.cloned.1.call-done, bf16[32,64]{1,0:T(8,128)(2,1)S(1)} %add_convert_fusion.1, bf16[32,8]{0,1:T(8,128)(2,1)S(1)} %get-tuple-element.5), kind=kOutput, calls=%fused_computation.18 | convolution fusion | flops 33669120 | bytes 1249792 | tf_op jit(solution)/shard_map/xpl,ply->xy/dot_general | solution.py:22
  71.1 0.4 fusion.52
  71.5 1.5 convolution_convert_fusion
  73.0 9.8 %fusion.17 = f32[32,8192]{1,0:T(8,128)} fusion(bf16[1024,8192]{1,0:T(8,128)(2,1)} %param.14, bf16[4,8,8,128]{3,2,1,0:T(8,128)(2,1)S(1)} %bitcast.54), kind=kOutput, calls=%fused_computation.24 | convolution fusion | flops 536870912 | bytes 17891328 | tf_op jit(solution)/shard_map/dot_general | solution.py:86
  82.9 1.8 %fusion.11 = f32[32,64]{1,0:T(8,128)S(1)} fusion(bf16[32,1024,1]{1,0,2:T(8,128)(2,1)S(1)} %reshape.106, bf16[8,64,1024]{2,1,0:T(8,128)(2,1)} %all-gather.9.cloned.1.call-done, f32[32,8]{0,1:T(8,128)S(1)} %get-tuple-element.6), kind=kOutput, calls=%fused_computation.17 | convolution fusion | flops 33585152 | bytes 1123328 | tf_op jit(solution)/shard_map/ah,fth->aft/dot_general | solution.py:15
  84.7 1.4 collective-permute-start.3
  86.1 2.4 %collective-permute-done.3 = f32[32,64]{1,0:T(8,128)S(1)} collective-permute-done((f32[32,64]{1,0:T(8,128)S(1)}, f32[32,64]{1,0:T(8,128)S(1)}, u32[]{:S(2)}, u32[]{:S(2)}) %collective-permute-start.3) | collective-permute-done | bytes 8224 | tf_op jit(solution)/shard_map/ppermute | solution.py:19
  88.5 2.0 %collective-permute-start.4 = (f32[32,64]{1,0:T(8,128)S(1)}, f32[32,64]{1,0:T(8,128)S(1)}, u32[]{:S(2)}, u32[]{:S(2)}) collective-permute-start(f32[32,64]{1,0:T(8,128)S(1)} %add.40), channel_id=1, source_target_pairs={{0,2},{1,3},{2,0},{3,1},{4,6},{5,7},{6,4},{7,5},{8,10},{9,11},{10,... | collective-permute-start | bytes 24584 | tf_op jit(solution)/shard_map/ppermute | solution.py:19
  90.5 1.7 %collective-permute-done.4 = f32[32,64]{1,0:T(8,128)S(1)} collective-permute-done((f32[32,64]{1,0:T(8,128)S(1)}, f32[32,64]{1,0:T(8,128)S(1)}, u32[]{:S(2)}, u32[]{:S(2)}) %collective-permute-start.4) | collective-permute-done | bytes 8224 | tf_op jit(solution)/shard_map/ppermute | solution.py:19
  92.2 2.2 %collective-permute-start.5 = (f32[32,64]{1,0:T(8,128)S(1)}, f32[32,64]{1,0:T(8,128)S(1)}, u32[]{:S(2)}, u32[]{:S(2)}) collective-permute-start(f32[32,64]{1,0:T(8,128)S(1)} %add.41), channel_id=1, source_target_pairs={{0,4},{1,5},{2,6},{3,7},{4,0},{5,1},{6,2},{7,3},{8,12},{9,13},{10,... | collective-permute-start | bytes 24584 | tf_op jit(solution)/shard_map/ppermute | solution.py:19
  94.5 2.4 %collective-permute-done.5 = f32[32,64]{1,0:T(8,128)S(1)} collective-permute-done((f32[32,64]{1,0:T(8,128)S(1)}, f32[32,64]{1,0:T(8,128)S(1)}, u32[]{:S(2)}, u32[]{:S(2)}) %collective-permute-start.5) | collective-permute-done | bytes 8224 | tf_op jit(solution)/shard_map/ppermute | solution.py:19
  96.9 51.0 %reduce-scatter.2.cloned.1.call-done = f32[32,1024]{1,0:T(8,128)} async-done(((f32[32,8192]{1,0:T(8,128)}), f32[32,1024]{1,0:T(8,128)}) %reduce-scatter.2.cloned.1.call-update) | async-done | bytes 131088 | tf_op jit(solution)/shard_map/reduce_scatter | solution.py:87
  148.0 2.2 %fusion.8 = bf16[32,1024]{1,0:T(8,128)(2,1)} fusion(f32[32,1024]{1,0:T(8,128)} %reduce-scatter.2.cloned.1.call-done, bf16[8,64,1024]{2,1,0:T(8,128)(2,1)} %all-gather.11.cloned.1.call-done, bf16[32,64]{1,0:T(8,128)(2,1)S(1)} %add_convert_fusion, bf16[32,8]{0,1:T(8,128)(2,1)S(1)} %get-tuple-element.5), kind=kOutput, calls=%fused_computation.13 | convolution fusion | flops 33669120 | bytes 1249792 | tf_op jit(solution)/shard_map/xpl,ply->xy/dot_general | solution.py:22
  (34 shorter events, 0.6 us)
Async XLA Ops:
  6.5 64.5 %copy-start = (bf16[32,8,32,128]{3,2,1,0:T(8,128)(2,1)S(1)}, bf16[32,8,32,128]{3,2,1,0:T(8,128)(2,1)}, u32[]{:S(2)}) copy-start(bf16[32,8,32,128]{3,2,1,0:T(8,128)(2,1)} %param.15) | copy-start | bytes 6291460
  6.5 2.9 %copy-start.4 = (s32[64]{0:T(128)S(1)}, s32[64]{0:T(128)}, u32[]{:S(2)}) copy-start(s32[64]{0:T(128)} %param.21) | copy-start | bytes 772
  6.5 2.9 %copy-start.3 = (s32[8]{0:T(128)S(1)}, s32[8]{0:T(128)}, u32[]{:S(2)}) copy-start(s32[8]{0:T(128)} %param.22) | copy-start | bytes 100
  6.5 14.1 %copy-start.1 = (bf16[32,1024]{1,0:T(8,128)(2,1)S(1)}, bf16[32,1024]{1,0:T(8,128)(2,1)}, u32[]{:S(2)}) copy-start(bf16[32,1024]{1,0:T(8,128)(2,1)} %param.12) | copy-start | bytes 196612
  6.5 14.1 %all-gather.5.cloned.1.call-start = ((), (), s32[]{:S(2)}) async-start(), calls=%async_computation.1 | async-start | bytes 1572864 | tf_op jit(solution)/shard_map/all_gather | solution.py:47
  7.3 62.1 %all-gather.7.cloned.1.call-start = ((), (), s32[]{:S(2)}) async-start(), calls=%async_computation.2 | async-start | bytes 1572864 | tf_op jit(solution)/shard_map/all_gather | solution.py:48
  8.0 74.8 %all-gather.9.cloned.1.call-start = ((), (), s32[]{:S(2)}) async-start(), calls=%async_computation.4 | async-start | bytes 1572864 | tf_op jit(solution)/shard_map/all_gather | solution.py:49
  8.8 88.2 %all-gather.11.cloned.1.call-start = ((), (), s32[]{:S(2)}) async-start(), calls=%async_computation.5 | async-start | bytes 1572864 | tf_op jit(solution)/shard_map/all_gather | solution.py:50
  9.3 138.6 %reduce-scatter.2.cloned.1.call-start = ((), (), s32[]{:S(2)}) async-start(), calls=%async_computation.3 | async-start | bytes 1179648 | tf_op jit(solution)/shard_map/reduce_scatter | solution.py:87
  22.5 33.3 %collective-permute-start = (f32[32,64]{1,0:T(8,128)S(1)}, f32[32,64]{1,0:T(8,128)S(1)}, u32[]{:S(2)}, u32[]{:S(2)}) collective-permute-start(f32[32,64]{1,0:T(8,128)S(1)} %fusion.10), channel_id=1, source_target_pairs={{0,1},{1,0},{2,3},{3,2},{4,5},{5,4},{6,7},{7,6},{8,9},{9,8},{10,11... | collective-permute-start | bytes 24584 | tf_op jit(solution)/shard_map/ppermute | solution.py:19
  55.8 10.1 %copy-start.2 = (s32[32]{0:T(128)S(1)}, s32[32]{0:T(128)}, u32[]{:S(2)}) copy-start(s32[32]{0:T(128)} %param.23) | copy-start | bytes 388
  55.9 8.8 %collective-permute-start.1 = (f32[32,64]{1,0:T(8,128)S(1)}, f32[32,64]{1,0:T(8,128)S(1)}, u32[]{:S(2)}, u32[]{:S(2)}) collective-permute-start(f32[32,64]{1,0:T(8,128)S(1)} %add.35), channel_id=1, source_target_pairs={{0,2},{1,3},{2,0},{3,1},{4,6},{5,7},{6,4},{7,5},{8,10},{9,11},{10,... | collective-permute-start | bytes 24584 | tf_op jit(solution)/shard_map/ppermute | solution.py:19
  64.7 4.7 %collective-permute-start.2 = (f32[32,64]{1,0:T(8,128)S(1)}, f32[32,64]{1,0:T(8,128)S(1)}, u32[]{:S(2)}, u32[]{:S(2)}) collective-permute-start(f32[32,64]{1,0:T(8,128)S(1)} %add.36), channel_id=1, source_target_pairs={{0,4},{1,5},{2,6},{3,7},{4,0},{5,1},{6,2},{7,3},{8,12},{9,13},{10,... | collective-permute-start | bytes 24584 | tf_op jit(solution)/shard_map/ppermute | solution.py:19
  84.7 3.8 %collective-permute-start.3 = (f32[32,64]{1,0:T(8,128)S(1)}, f32[32,64]{1,0:T(8,128)S(1)}, u32[]{:S(2)}, u32[]{:S(2)}) collective-permute-start(f32[32,64]{1,0:T(8,128)S(1)} %fusion.11), channel_id=1, source_target_pairs={{0,1},{1,0},{2,3},{3,2},{4,5},{5,4},{6,7},{7,6},{8,9},{9,8},{10,11... | collective-permute-start | bytes 24584 | tf_op jit(solution)/shard_map/ppermute | solution.py:19
  88.5 3.7 %collective-permute-start.4 = (f32[32,64]{1,0:T(8,128)S(1)}, f32[32,64]{1,0:T(8,128)S(1)}, u32[]{:S(2)}, u32[]{:S(2)}) collective-permute-start(f32[32,64]{1,0:T(8,128)S(1)} %add.40), channel_id=1, source_target_pairs={{0,2},{1,3},{2,0},{3,1},{4,6},{5,7},{6,4},{7,5},{8,10},{9,11},{10,... | collective-permute-start | bytes 24584 | tf_op jit(solution)/shard_map/ppermute | solution.py:19
  92.2 4.7 %collective-permute-start.5 = (f32[32,64]{1,0:T(8,128)S(1)}, f32[32,64]{1,0:T(8,128)S(1)}, u32[]{:S(2)}, u32[]{:S(2)}) collective-permute-start(f32[32,64]{1,0:T(8,128)S(1)} %add.41), channel_id=1, source_target_pairs={{0,4},{1,5},{2,6},{3,7},{4,0},{5,1},{6,2},{7,3},{8,12},{9,13},{10,... | collective-permute-start | bytes 24584 | tf_op jit(solution)/shard_map/ppermute | solution.py:19
Sparse Core Ops, SparseCore 0:
  8.9 11.7 all-gather.4
  22.2 10.1 all-gather.6
  34.0 10.1 all-gather.8
  45.6 10.1 all-gather.10
  82.9 65.0 reduce-scatter.1
